TPU v7x, 256 devices: a whole 4x4x8 slice. The times are simulated.
256 devices in a mesh: vertex: 16 (over z, core), tm: 16 (over y, x).
Axes of the slice: x: 4, y: 4, z: 8, core: 2. Of those that a mesh axis runs over, the one named last changes fastest.
Arguments:
- features: bfloat16 [16, 16384, 512], P('tm', 'vertex'), may hold values from -6 to 6
- tile_coord: int32 [16, 2048, 2], P('tm', 'vertex'), may hold values from 0 to 127, as said below
- tile_count: int32 [16, 16], P('tm', 'vertex'), may hold values from 1 to 128, as said below
- tile_values: bfloat16 [16, 2048, 128, 128], P('tm', 'vertex'), may hold values from -0.125 to 0.125
- w_agg: bfloat16 [512, 512], replicated, may hold values from -0.25 to 0.25
- w_root: bfloat16 [512, 512], replicated, may hold values from -0.25 to 0.25
- time_embed: bfloat16 [16, 512], replicated, may hold values from -6 to 6
- gain_first: bfloat16 [512], replicated, may hold values from 0.25 to 1.75
- w_qkv: bfloat16 [512, 1536], replicated, may hold values from -12 to 12
- w_out: bfloat16 [512, 512], replicated, may hold values from -0.25 to 0.25
- gain_second: bfloat16 [512], replicated, may hold values from 0.25 to 1.75
- w_up: bfloat16 [512, 1024], replicated, may hold values from -0.25 to 0.25
- w_down: bfloat16 [1024, 512], replicated, may hold values from -0.1875 to 0.1875
Outputs:
- layer_out: bfloat16 [16, 16384, 512], P(None, ('vertex', 'tm'))
Inputs may be any that keep to these rules, and one draw needn't show every extreme that they name: `tile_coord`: entry 0 of a slot is a row block 0 to 7 of the device's own vertices, entry 1 a column block 0 to 127; no pair repeats among one device's 128 slots, live or not. `tile_count`: live slots are the first ones of a device; in every snapshot some device has all 128 slots live.
All inputs are finite; a program needn't handle non-finite values.
Results may differ from a plain program's by a relative error of at most 0.006.
Values may be sent and summed in bfloat16 or wider, within the bound.
No kernel may reach another device: no remote copies, remote signals or barrier semaphores. Data moves between devices by JAX's collectives and lax.ppermute only.
A program may use at most 192 MiB of HBM per device.

v0:
```python
import math
import jax
import jax.numpy as jnp
from jax import lax
from jax.sharding import PartitionSpec as P

HEADS = 8


def norm_rows(values, gain):
    scale = lax.rsqrt(jnp.mean(values * values, axis=-1, keepdims=True) + 1e-06)
    return values * scale * gain.astype(jnp.float32)


def project(left, right):
    return jnp.einsum("sid,de->sie", left, right, preferred_element_type=jnp.float32)


def temporal(graph_rows, time_embed, gain_first, w_qkv, w_out, gain_second, w_up, w_down):
    snap_count, item_count, width = graph_rows.shape
    head_size = width // HEADS
    mixed = graph_rows.astype(jnp.float32) + time_embed.astype(jnp.float32)[:, None, :]
    normed = norm_rows(mixed, gain_first).astype(jnp.bfloat16)
    qkv = project(normed, w_qkv).astype(jnp.bfloat16)
    query = qkv[..., :width].reshape(snap_count, item_count, HEADS, head_size)
    key_rows = qkv[..., width : 2 * width].reshape(snap_count, item_count, HEADS, head_size)
    value_rows = qkv[..., 2 * width :].reshape(snap_count, item_count, HEADS, head_size)
    scores = jnp.einsum(
        "sihd,tihd->ihst", query, key_rows, preferred_element_type=jnp.float32
    ) / math.sqrt(head_size)
    causal = jnp.arange(snap_count)[:, None] >= jnp.arange(snap_count)[None, :]
    scores = jnp.where(causal, scores, -1e30)
    largest = jnp.max(scores, axis=-1, keepdims=True)
    expo = jnp.where(causal, jnp.exp(scores - largest), 0.0)
    weights_soft = (expo / jnp.sum(expo, axis=-1, keepdims=True)).astype(jnp.bfloat16)
    context = jnp.einsum(
        "ihst,tihd->sihd", weights_soft, value_rows, preferred_element_type=jnp.float32
    )
    context = context.astype(jnp.bfloat16).reshape(snap_count, item_count, width)
    residual = mixed + project(context, w_out)
    normed_two = norm_rows(residual, gain_second).astype(jnp.bfloat16)
    hidden = jax.nn.gelu(project(normed_two, w_up)).astype(jnp.bfloat16)
    return (residual + project(hidden, w_down)).astype(jnp.bfloat16)


def per_device(
    features,
    tile_coord,
    tile_count,
    tile_values,
    w_agg,
    w_root,
    time_embed,
    gain_first,
    w_qkv,
    w_out,
    gain_second,
    w_up,
    w_down,
):
    own_rows = features[0]
    tile_pairs = tile_coord[0]
    live_count = tile_count[0, 0]
    tile_block = tile_values[0]
    local_vertices, width = own_rows.shape
    tile_size = tile_block.shape[1]
    row_blocks = local_vertices // tile_size
    slot_count = tile_block.shape[0]
    alive = jnp.arange(slot_count) < live_count
    gathered = lax.all_gather(own_rows, "vertex", axis=0, tiled=True)
    blocks = gathered.reshape(-1, tile_size, width)
    chosen = blocks[tile_pairs[:, 1]]
    products = jnp.einsum("tij,tjd->tid", tile_block, chosen, preferred_element_type=jnp.float32)
    products = jnp.where(alive[:, None, None], products, 0.0)
    summed = jax.ops.segment_sum(products, tile_pairs[:, 0], num_segments=row_blocks)
    summed = summed.reshape(local_vertices, width)
    neighbor_sum = summed.astype(jnp.bfloat16)
    combined = jnp.dot(neighbor_sum, w_agg, preferred_element_type=jnp.float32)
    combined = combined + jnp.dot(own_rows, w_root, preferred_element_type=jnp.float32)
    graph_rows = jax.nn.gelu(combined).astype(jnp.bfloat16)
    tm_count = lax.axis_size("tm")
    sectioned = graph_rows.reshape(1, tm_count, local_vertices // tm_count, width)
    mixed_out = temporal(
        lax.all_to_all(sectioned, "tm", split_axis=1, concat_axis=0, tiled=True)[:, 0],
        time_embed,
        gain_first,
        w_qkv,
        w_out,
        gain_second,
        w_up,
        w_down,
    )
    result = mixed_out[:, None]
    return result[:, 0]


def solution(mesh):
    return jax.shard_map(
        per_device,
        mesh=mesh,
        in_specs=(
            P("tm", "vertex", None),
            P("tm", "vertex", None),
            P("tm", "vertex"),
            P("tm", "vertex", None, None),
            P(),
            P(),
            P(),
            P(),
            P(),
            P(),
            P(),
            P(),
            P(),
        ),
        out_specs=P(None, ("vertex", "tm"), None),
        check_vma=False,
    )
```

profile of v0, /device:TPU:1, one launch (start us, length us, event | category | flops | bytes accessed | tf_op | source)
XLA Modules:
  0.0 339.0 jit_solution(8120423000765595668)
XLA Ops:
  8.7 100.1 %all-gather.3.cloned.1.call-done = bf16[1,16384,512]{2,1,0:T(8,128)(2,1)} async-done(((bf16[1,1024,512]{2,1,0:T(8,128)(2,1)}), bf16[1,16384,512]{2,1,0:T(8,128)(2,1)}) %all-gather.3.cloned.1.call-update) | async-done | bytes 16777232 | tf_op jit(solution)/shard_map/all_gather | solution.py:70
  108.7 14.1 %gather_fusion = bf16[128,128,512]{2,1,0:T(8,128)(2,1)} fusion(bf16[128,128,512]{2,1,0:T(8,128)(2,1)} %bitcast.55, s32[1024]{0:T(1024)S(1)} %pad_clamp_fusion), kind=kCustom, calls=%fused_computation | custom fusion | bytes 33554944 | tf_op jit(solution)/shard_map/gather | solution.py:72
  122.8 22.4 %select_bitcast_fusion = f32[128,128,512]{1,2,0:T(8,128)} fusion(pred[128]{0:T(512)(128)(4,1)S(1)} %iota_compare_fusion.1, bf16[128,128,512]{2,1,0:T(8,128)(2,1)} %gather_fusion, bf16[1,128,128,128]{3,2,1,0:T(8,128)(2,1)} %param.16), kind=kOutput, calls=%fused_computation.3 | convolution fusion | flops 2155872256 | bytes 54526080 | tf_op jit(solution)/shard_map/tij,tjd->tid/dot_general | solution.py:73
  145.2 33.5 %copy.36 = f32[128,128,512]{2,1,0:T(8,128)} copy(f32[128,128,512]{1,2,0:T(8,128)} %select_bitcast_fusion) | data formatting | bytes 67108864 | tf_op jit(solution)/shard_map/jit(_where)/select_n | solution.py:74
  178.7 1.6 broadcast_in_dim.40
  180.3 69.9 %scatter_fusion = f32[8,128,512]{2,1,0:T(8,128)} fusion(f32[8,128,512]{2,1,0:T(8,128)} %broadcast_in_dim.40, s32[128]{0:T(128)S(1)} %get-tuple-element.9, f32[128,128,512]{2,1,0:T(8,128)} %copy.36), kind=kCustom, calls=%fused_computation.1 | custom fusion | flops 8388608 | bytes 100663808 | tf_op jit(solution)/shard_map/scatter-add | solution.py:75
  250.2 1.8 convert_element_type.48
  253.3 2.1 fusion.17
  255.5 7.0 %all-to-all-start = ((bf16[1,16,64,512]{3,2,0,1:T(8,128)(2,1)}), bf16[1,16,64,512]{3,2,0,1:T(8,128)(2,1)S(1)}, u32[]{:S(2)}, u32[]{:S(2)}) async-start(bf16[1,16,64,512]{3,2,0,1:T(8,128)(2,1)} %bitcast.57), calls=%async_computation | async-start | bytes 2097152 | tf_op jit(solution)/shard_map/all_to_all | solution.py:84
  262.5 16.4 %all-to-all-done = bf16[1,16,64,512]{3,2,0,1:T(8,128)(2,1)S(1)} async-done(((bf16[1,16,64,512]{3,2,0,1:T(8,128)(2,1)}), bf16[1,16,64,512]{3,2,0,1:T(8,128)(2,1)S(1)}, u32[]{:S(2)}, u32[]{:S(2)}) %all-to-all-start) | async-done | bytes 1048608 | tf_op jit(solution)/shard_map/all_to_all | solution.py:84
  279.3 1.9 convolution_convert_fusion
  281.1 1.8 fusion.60
  282.9 3.9 %reshape.54 = bf16[16,64,8,64]{3,2,1,0:T(8,128)(2,1)} reshape(bf16[16,64,512]{2,1,0:T(8,128)(2,1)} %get-tuple-element.7) | data formatting | bytes 2097152 | tf_op jit(solution)/shard_map/reshape | solution.py:25
  286.8 3.9 %reshape.55 = bf16[16,64,8,64]{3,2,1,0:T(8,128)(2,1)} reshape(bf16[16,64,512]{2,1,0:T(8,128)(2,1)} %get-tuple-element.6) | data formatting | bytes 2097152 | tf_op jit(solution)/shard_map/reshape | solution.py:26
  290.7 6.7 %fusion.26 = f32[64,8,16,16]{2,3,1,0:T(8,128)} fusion(bf16[16,64,8,64]{3,2,1,0:T(8,128)(2,1)} %reshape.55, bf16[16,64,8,64]{3,2,1,0:T(8,128)(2,1)} %reshape.54), kind=kOutput, calls=%fused_computation.33 | convolution fusion | flops 16777216 | bytes 2621440 | tf_op jit(solution)/shard_map/sihd,tihd->ihst/dot_general | solution.py:28
  297.4 4.7 %copy.41 = f32[64,8,16,16]{0,3,2,1:T(8,128)} copy(f32[64,8,16,16]{2,3,1,0:T(8,128)} %fusion.26) | data formatting | bytes 1048576 | tf_op jit(solution)/shard_map/sihd,tihd->ihst/dot_general | solution.py:28
  302.1 2.6 fusion.61
  304.9 3.9 %copy.43 = bf16[64,8,16,16]{3,2,1,0:T(8,128)(2,1)} copy(bf16[64,8,16,16]{0,3,2,1:T(8,128)(2,1)S(1)} %divide_convert_fusion) | data formatting | bytes 524288 | tf_op jit(solution)/shard_map/convert_element_type | solution.py:35
  308.8 3.9 %reshape.53 = bf16[16,64,8,64]{3,2,1,0:T(8,128)(2,1)} reshape(bf16[16,64,512]{2,1,0:T(8,128)(2,1)} %get-tuple-element.5) | data formatting | bytes 2097152 | tf_op jit(solution)/shard_map/reshape | solution.py:27
  312.7 3.7 %convert_bitcast_fusion = bf16[16,64,8,64]{3,0,2,1:T(8,128)(2,1)S(1)} fusion(bf16[64,8,16,16]{3,2,1,0:T(8,128)(2,1)} %copy.43, bf16[16,64,8,64]{3,2,1,0:T(8,128)(2,1)} %reshape.53), kind=kOutput, calls=%fused_computation.39 | convolution fusion | flops 17301504 | bytes 2359296 | tf_op jit(solution)/shard_map/ihst,tihd->sihd/dot_general | solution.py:36
  316.4 1.9 copy.44
  318.3 4.0 %reshape.56 = bf16[16,64,512]{2,1,0:T(8,128)(2,1)} reshape(bf16[16,64,8,64]{3,2,1,0:T(8,128)(2,1)} %copy.44) | data formatting | bytes 2097152 | tf_op jit(solution)/shard_map/reshape | solution.py:39
  322.4 3.5 %multiply_reduce_fusion = (f32[16,64]{1,0:T(8,128)S(1)}, f32[16,64,512]{2,1,0:T(8,128)}) fusion(bf16[16,64,512]{2,1,0:T(8,128)(2,1)} %reshape.56, bf16[512,512]{1,0:T(8,128)(2,1)} %param.22, f32[16,512]{1,0:T(8,128)S(1)} %convert_element_type.53, bf16[1,16,64,512]{3,2,0,1:T(8,128)(2,1)S(1)} %all-to-all-done), kind=kOutput, calls=%fused_computation.38 | convolution fusion | flops 539491328 | bytes 4755456 | tf_op jit(solution)/shard_map/sid,de->sie/dot_general | solution.py:16
  325.8 6.3 %add_convert_fusion = bf16[16,64,512]{2,1,0:T(8,128)(2,1)} fusion(f32[16,64,512]{2,1,0:T(8,128)} %get-tuple-element.13, bf16[1024,512]{1,0:T(8,128)(2,1)} %param.25, bf16[512,1024]{1,0:T(8,128)(2,1)} %param.24, f32[512]{0:T(512)S(1)} %convert_element_type.60, f32[16,64]{1,0:T(8,128)S(1)} %add_rsqrt_fusion), kind=kOutput, calls=%fused_computation.36 | convolution fusion | flops 2159542272 | bytes 5249024 | tf_op jit(solution)/shard_map/sid,de->sie/dot_general | solution.py:16
  (28 shorter events, 3.3 us)
Async XLA Ops:
  6.5 272.7 %copy-start = (bf16[512,1536]{1,0:T(8,128)(2,1)S(1)}, bf16[512,1536]{1,0:T(8,128)(2,1)}, u32[]{:S(2)}) copy-start(bf16[512,1536]{1,0:T(8,128)(2,1)} %param.21) | copy-start | bytes 4718596
  6.5 102.2 %all-gather.3.cloned.1.call-start = ((), (), s32[]{:S(2)}) async-start(), calls=%async_computation.1 | async-start | bytes 17825792 | tf_op jit(solution)/shard_map/all_gather | solution.py:70
  250.2 1.8 copy-start.2
  252.0 1.2 copy-start.1
  252.0 1.3 copy-start.6
  255.4 7.0 %copy-start.3 = (bf16[16,512]{1,0:T(8,128)(2,1)S(1)}, bf16[16,512]{1,0:T(8,128)(2,1)}, u32[]{:S(2)}) copy-start(bf16[16,512]{1,0:T(8,128)(2,1)} %param.19) | copy-start | bytes 49156
  255.5 7.0 %copy-start.4 = (bf16[512]{0:T(512)(128)(2,1)S(1)}, bf16[512]{0:T(512)(128)(2,1)}, u32[]{:S(2)}) copy-start(bf16[512]{0:T(512)(128)(2,1)} %param.20) | copy-start | bytes 3076
  255.5 7.0 %copy-start.5 = (bf16[512]{0:T(512)(128)(2,1)S(1)}, bf16[512]{0:T(512)(128)(2,1)}, u32[]{:S(2)}) copy-start(bf16[512]{0:T(512)(128)(2,1)} %param.23) | copy-start | bytes 3076
  255.5 23.5 %all-to-all-start = ((bf16[1,16,64,512]{3,2,0,1:T(8,128)(2,1)}), bf16[1,16,64,512]{3,2,0,1:T(8,128)(2,1)S(1)}, u32[]{:S(2)}, u32[]{:S(2)}) async-start(bf16[1,16,64,512]{3,2,0,1:T(8,128)(2,1)} %bitcast.57), calls=%async_computation | async-start | bytes 2097152 | tf_op jit(solution)/shard_map/all_to_all | solution.py:84
Sparse Core Ops, SparseCore 0:
  9.2 99.5 all-gather.2
where the time goes:
time: 340 us; the launch traced here: 339 us
  waiting for transfers between devices  117 us (34%)
  local copies, waits for them, and re-layouts  77.8 us (23%)
  other arithmetic  75.6 us (22%)
  matrix products  47.3 us (14%)
  between operations  14.2 us (4%)
  starting transfers between devices  6.97 us (2%)
    all_gather x1, waiting for transfers between devices, per_device(): gathered = lax.all_gather(own_rows, 'vertex', axis=0, tiled=True)  100 us
    scatter-add x1, other arithmetic, per_device(): jax.ops.segment_sum(products, tile_pairs[:, 0], num_segments=row_blocks)  69.9 us
    select_n x1, local copies, waits for them, and re-layouts, per_device(): products = jnp.where(alive[:, None, None], products, 0.0)  33.5 us
    dot_general x1, matrix products, per_device(): jnp.einsum('tij,tjd->tid', tile_block, chosen, preferred_element_type=jnp...  22.4 us
    all_to_all x1, waiting for transfers between devices, per_device(): lax.all_to_all(sectioned, 'tm', split_axis=1, concat_axis=0, tiled=True)  16.4 us
    gather x1, local copies, waits for them, and re-layouts, per_device(): chosen = blocks[tile_pairs[:, 1]]  14.1 us
    dot_general x3, matrix products, project(): jnp.einsum('sid,de->sie', left, right, preferred_element_type=jnp.float32)  11.6 us
    all_to_all x1, starting transfers between devices, per_device(): lax.all_to_all(sectioned, 'tm', split_axis=1, concat_axis=0, tiled=True)  6.97 us
  transfers between devices with their start and end apart: 2, of which 2 were waited for; matrix products, arithmetic and copies ran while one was open for 0% of the time, Pallas kernels for 0%

commit v1 on v0

--- a/solution.py
+++ b/solution.py
@@ -3,6 +3,7 @@
 import jax.numpy as jnp
 from jax import lax
 from jax.sharding import PartitionSpec as P
+from jax.lax import all_to_all, axis_size
 
 HEADS = 8
 
@@ -67,7 +68,11 @@
     row_blocks = local_vertices // tile_size
     slot_count = tile_block.shape[0]
     alive = jnp.arange(slot_count) < live_count
-    gathered = lax.all_gather(own_rows, "vertex", axis=0, tiled=True)
+    in_order = []
+    for _ in range(axis_size("vertex")):
+        in_order.append(own_rows)
+    top = jnp.concatenate(in_order, axis=0)
+    gathered = all_to_all(top, "vertex", split_axis=0, concat_axis=0, tiled=True)
     blocks = gathered.reshape(-1, tile_size, width)
     chosen = blocks[tile_pairs[:, 1]]
     products = jnp.einsum("tij,tjd->tid", tile_block, chosen, preferred_element_type=jnp.float32)

time: 340 us -> 608 us (1.79)
  waiting for transfers between devices: 117 us -> 378 us
  between operations: 14.2 us -> 0.99 us
  starting transfers between devices: 6.97 us -> 17.2 us
  local copies, waits for them, and re-layouts: 77.8 us -> 86.6 us
    all_to_all x0 -> x1, waiting for transfers between devices: none -> 362 us  [per_device(): all_to_all(top, 'vertex', split_axis=0, concat_axis=0, tiled=True)]
    all_gather x1 -> x0, waiting for transfers between devices: 100 us -> none  [per_device(): gathered = lax.all_gather(own_rows, 'vertex', axis=0, tiled=True)]
    all_to_all x0 -> x1, starting transfers between devices: none -> 10.1 us  [per_device(): all_to_all(top, 'vertex', split_axis=0, concat_axis=0, tiled=True)]
    unnamed x14 -> x35, local copies, waits for them, and re-layouts: 0.65 us -> 9.39 us
where the time goes in v1:
time: 608 us; the launch traced here: 605 us
  waiting for transfers between devices  378 us (62%)
  local copies, waits for them, and re-layouts  86.6 us (14%)
  other arithmetic  74.8 us (12%)
  matrix products  47.2 us (8%)
  starting transfers between devices  17.2 us (3%)
    all_to_all x1, waiting for transfers between devices, per_device(): all_to_all(top, 'vertex', split_axis=0, concat_axis=0, tiled=True)  362 us
    scatter-add x1, other arithmetic, per_device(): jax.ops.segment_sum(products, tile_pairs[:, 0], num_segments=row_blocks)  69.8 us
    select_n x1, local copies, waits for them, and re-layouts, per_device(): products = jnp.where(alive[:, None, None], products, 0.0)  33.4 us
    dot_general x1, matrix products, per_device(): jnp.einsum('tij,tjd->tid', tile_block, chosen, preferred_element_type=jnp...  22.5 us
    all_to_all x1, waiting for transfers between devices, per_device(): lax.all_to_all(sectioned, 'tm', split_axis=1, concat_axis=0, tiled=True)  15.8 us
    gather x1, local copies, waits for them, and re-layouts, per_device(): chosen = blocks[tile_pairs[:, 1]]  14.1 us
  transfers between devices with their start and end apart: 2, of which 2 were waited for; matrix products, arithmetic and copies ran while one was open for 0% of the time, Pallas kernels for 0%

profile of v1, /device:TPU:1, one launch (start us, length us, event | category | flops | bytes accessed | tf_op | source)
XLA Modules:
  0.0 605.0 jit_solution(6932218908597695649)
XLA Ops:
  3.9 5.7 copy-done.2
  9.6 10.1 %all-to-all-start = ((bf16[16,1024,512]{2,1,0:T(8,128)(2,1)}), bf16[16,1024,512]{2,1,0:T(8,128)(2,1)}, u32[]{:S(2)}, u32[]{:S(2)}) async-start(bf16[16,1024,512]{2,1,0:T(8,128)(2,1)} %bitcast.72), calls=%async_computation | async-start | bytes 33554432 | tf_op jit(solution)/shard_map/all_to_all | solution.py:75
  20.4 362.4 %all-to-all-done = bf16[16,1024,512]{2,1,0:T(8,128)(2,1)} async-done(((bf16[16,1024,512]{2,1,0:T(8,128)(2,1)}), bf16[16,1024,512]{2,1,0:T(8,128)(2,1)}, u32[]{:S(2)}, u32[]{:S(2)}) %all-to-all-start) | async-done | bytes 16777248 | tf_op jit(solution)/shard_map/all_to_all | solution.py:75
  382.7 14.1 %gather_fusion = bf16[128,128,512]{2,1,0:T(8,128)(2,1)} fusion(bf16[128,128,512]{2,1,0:T(8,128)(2,1)} %bitcast.5, s32[1024]{0:T(1024)S(1)} %pad_clamp_fusion), kind=kCustom, calls=%fused_computation | custom fusion | bytes 33554944 | tf_op jit(solution)/shard_map/gather | solution.py:77
  396.8 22.5 %select_bitcast_fusion = f32[128,128,512]{1,2,0:T(8,128)} fusion(pred[128]{0:T(512)(128)(4,1)S(1)} %iota_compare_fusion.1, bf16[128,128,512]{2,1,0:T(8,128)(2,1)} %gather_fusion, bf16[1,128,128,128]{3,2,1,0:T(8,128)(2,1)} %param.16), kind=kOutput, calls=%fused_computation.3 | convolution fusion | flops 2155872256 | bytes 54526080 | tf_op jit(solution)/shard_map/tij,tjd->tid/dot_general | solution.py:78
  419.3 33.4 %copy.36 = f32[128,128,512]{2,1,0:T(8,128)} copy(f32[128,128,512]{1,2,0:T(8,128)} %select_bitcast_fusion) | data formatting | bytes 67108864 | tf_op jit(solution)/shard_map/jit(_where)/select_n | solution.py:79
  454.3 69.8 %scatter_fusion = f32[8,128,512]{2,1,0:T(8,128)} fusion(f32[8,128,512]{2,1,0:T(8,128)} %broadcast_in_dim.40, s32[128]{0:T(128)S(1)} %get-tuple-element.9, f32[128,128,512]{2,1,0:T(8,128)} %copy.36), kind=kCustom, calls=%fused_computation.1 | custom fusion | flops 8388608 | bytes 100663808 | tf_op jit(solution)/shard_map/scatter-add | solution.py:80
  524.1 1.8 convert_element_type.48
  526.7 2.1 fusion.17
  528.8 7.1 %all-to-all-start.1 = ((bf16[1,16,64,512]{3,2,0,1:T(8,128)(2,1)}), bf16[1,16,64,512]{3,2,0,1:T(8,128)(2,1)S(1)}, u32[]{:S(2)}, u32[]{:S(2)}) async-start(bf16[1,16,64,512]{3,2,0,1:T(8,128)(2,1)} %bitcast.74), calls=%async_computation.1 | async-start | bytes 2097152 | tf_op jit(solution)/shard_map/all_to_all | solution.py:89
  536.0 15.8 %all-to-all-done.1 = bf16[1,16,64,512]{3,2,0,1:T(8,128)(2,1)S(1)} async-done(((bf16[1,16,64,512]{3,2,0,1:T(8,128)(2,1)}), bf16[1,16,64,512]{3,2,0,1:T(8,128)(2,1)S(1)}, u32[]{:S(2)}, u32[]{:S(2)}) %all-to-all-start.1) | async-done | bytes 1048608 | tf_op jit(solution)/shard_map/all_to_all | solution.py:89
  552.2 1.9 convolution_convert_fusion
  555.8 3.9 reshape.57
  559.7 3.9 reshape.58
  563.6 6.7 %fusion.26 = f32[64,8,16,16]{2,3,1,0:T(8,128)} fusion(bf16[16,64,8,64]{3,2,1,0:T(8,128)(2,1)} %reshape.58, bf16[16,64,8,64]{3,2,1,0:T(8,128)(2,1)} %reshape.57), kind=kOutput, calls=%fused_computation.33 | convolution fusion | flops 16777216 | bytes 2621440 | tf_op jit(solution)/shard_map/sihd,tihd->ihst/dot_general | solution.py:29
  570.4 4.7 copy.41
  575.1 2.7 fusion.61
  577.9 3.9 copy.43
  581.8 3.9 reshape.56
  585.7 3.7 convert_bitcast_fusion
  589.5 1.9 copy.44
  591.3 4.0 reshape.59
  595.4 3.3 multiply_reduce_fusion
  598.7 6.3 %add_convert_fusion = bf16[16,64,512]{2,1,0:T(8,128)(2,1)} fusion(f32[16,64,512]{2,1,0:T(8,128)} %get-tuple-element.13, bf16[1024,512]{1,0:T(8,128)(2,1)} %param.25, bf16[512,1024]{1,0:T(8,128)(2,1)} %param.24, f32[512]{0:T(512)S(1)} %convert_element_type.60, f32[16,64]{1,0:T(8,128)S(1)} %add_rsqrt_fusion), kind=kOutput, calls=%fused_computation.36 | convolution fusion | flops 2159542272 | bytes 5249024 | tf_op jit(solution)/shard_map/sid,de->sie/dot_general | solution.py:17
  (49 shorter events, 8.3 us)
Async XLA Ops:
  0.0 552.2 %copy-start = (bf16[512,1536]{1,0:T(8,128)(2,1)S(1)}, bf16[512,1536]{1,0:T(8,128)(2,1)}, u32[]{:S(2)}) copy-start(bf16[512,1536]{1,0:T(8,128)(2,1)} %param.21) | copy-start | bytes 4718596
  0.0 2.7 copy-start.1
  3.9 5.7 copy-start.2
  9.6 10.8 %copy-start.7 = (s32[1,128,2]{1,2,0:T(2,128)S(1)}, s32[1,128,2]{1,2,0:T(2,128)}, u32[]{:S(2)}) copy-start(s32[1,128,2]{1,2,0:T(2,128)} %param.14) | copy-start | bytes 3076
  9.6 373.2 %all-to-all-start = ((bf16[16,1024,512]{2,1,0:T(8,128)(2,1)}), bf16[16,1024,512]{2,1,0:T(8,128)(2,1)}, u32[]{:S(2)}, u32[]{:S(2)}) async-start(bf16[16,1024,512]{2,1,0:T(8,128)(2,1)} %bitcast.72), calls=%async_computation | async-start | bytes 33554432 | tf_op jit(solution)/shard_map/all_to_all | solution.py:75
  454.3 71.6 %copy-start.3 = (bf16[512,512]{1,0:T(8,128)(2,1)S(1)}, bf16[512,512]{1,0:T(8,128)(2,1)}, u32[]{:S(2)}) copy-start(bf16[512,512]{1,0:T(8,128)(2,1)} %param.17) | copy-start | bytes 1572868
  524.1 2.5 copy-start.8
  526.7 9.3 %copy-start.4 = (bf16[16,512]{1,0:T(8,128)(2,1)S(1)}, bf16[16,512]{1,0:T(8,128)(2,1)}, u32[]{:S(2)}) copy-start(bf16[16,512]{1,0:T(8,128)(2,1)} %param.19) | copy-start | bytes 49156
  526.7 9.3 %copy-start.5 = (bf16[512]{0:T(512)(128)(2,1)S(1)}, bf16[512]{0:T(512)(128)(2,1)}, u32[]{:S(2)}) copy-start(bf16[512]{0:T(512)(128)(2,1)} %param.20) | copy-start | bytes 3076
  526.7 9.3 %copy-start.6 = (bf16[512]{0:T(512)(128)(2,1)S(1)}, bf16[512]{0:T(512)(128)(2,1)}, u32[]{:S(2)}) copy-start(bf16[512]{0:T(512)(128)(2,1)} %param.23) | copy-start | bytes 3076
  528.8 23.0 %all-to-all-start.1 = ((bf16[1,16,64,512]{3,2,0,1:T(8,128)(2,1)}), bf16[1,16,64,512]{3,2,0,1:T(8,128)(2,1)S(1)}, u32[]{:S(2)}, u32[]{:S(2)}) async-start(bf16[1,16,64,512]{3,2,0,1:T(8,128)(2,1)} %bitcast.74), calls=%async_computation.1 | async-start | bytes 2097152 | tf_op jit(solution)/shard_map/all_to_all | solution.py:89
  589.4 5.9 copy-start.9
